TPU v7x, 32 devices: a whole 2x2x4 slice. The times are simulated.
32 devices in a mesh: dp: 4 (over y, x), seq: 4 (over z), expert: 2 (over core).
Axes of the slice: x: 2, y: 2, z: 4, core: 2. Of those that a mesh axis runs over, the one named last changes fastest.
Arguments:
- queries: bfloat16 [8, 512, 2048], P(('dp', 'expert'), 'seq'), may hold values from -135 to 135
- keys: bfloat16 [8, 512, 2048], P(('dp', 'expert'), 'seq'), may hold values from -5 to 5
- values: bfloat16 [8, 512, 2048], P(('dp', 'expert'), 'seq'), may hold values from -6 to 6
- resid: bfloat16 [8, 512, 2048], P(('dp', 'expert'), 'seq'), may hold values from -20 to 20
- cotangent: bfloat16 [8, 512, 2048], P(('dp', 'expert'), 'seq'), may hold values from -0.3125 to 0.3125
- zone_ids: int32 [8, 512, 1], P(('dp', 'expert'), 'seq'), may hold values from 0 to 7; in each aligned block of 128 rows (0 to 127, 128 to 255, ..., all dimensions but the last counted through in order) at most 34 rows name the same one
- norm_gain: float32 [2048], replicated, may hold values from 0.1 to 1.9
- w_in: bfloat16 [8, 2048, 4096], P(('seq', 'expert'), None, 'dp'), may hold values from -0.125 to 0.125
- w_out: bfloat16 [8, 4096, 2048], P(('seq', 'expert'), 'dp'), may hold values from -0.09375 to 0.09375
Outputs:
- layer_out: bfloat16 [8, 512, 2048], P(('dp', 'expert'), 'seq')
- grad_w_in: bfloat16 [8, 2048, 4096], P(('seq', 'expert'), None, 'dp')
- grad_w_out: bfloat16 [8, 4096, 2048], P(('seq', 'expert'), 'dp')
Inputs may be any that keep to these rules, and one draw needn't show every extreme that they name: `zone_ids`: among the tokens of one device at most 34 name the same expert, and that count is reached.
All inputs are finite; a program needn't handle non-finite values.
Results may differ from a plain program's by a relative error of at most 0.0085.
Values may be sent and summed in bfloat16 or wider, within the bound.
A program may use at most 128 MiB of HBM per device.

v0:
```python
import math
import jax
import jax.numpy as jnp
from jax import lax
from jax.sharding import PartitionSpec as P

HEADS = 16
epsilon = 1e-05


def shards(queries, keys, values, resid, cotangent, zone_ids, norm_gain, w_in, w_out):
    local_rows = queries.shape[1]
    model_width = queries.shape[2]
    head_dim = model_width // HEADS
    score_scale = 1.0 / math.sqrt(head_dim)
    q_heads = queries[0].reshape(local_rows, HEADS, head_dim)
    peak_now = jnp.full((HEADS, local_rows), -jnp.inf, jnp.float32)
    totals = jnp.zeros((HEADS, local_rows), jnp.float32)
    accum = jnp.zeros((HEADS, local_rows, head_dim), jnp.float32)
    key_block = lax.all_gather(keys, "seq", axis=1, tiled=True)
    value_block = lax.all_gather(values, "seq", axis=1, tiled=True)
    count = key_block.shape[1]
    k_heads = key_block[0].reshape(count, HEADS, head_dim)
    v_heads = value_block[0].reshape(count, HEADS, head_dim)
    scores = (
        jnp.einsum("shd,thd->hst", q_heads, k_heads, preferred_element_type=jnp.float32)
        * score_scale
    )
    newest = jnp.max(scores, axis=-1)
    factor = jnp.exp(peak_now - newest)
    weights = jnp.exp(scores - newest[..., None])
    totals = totals * factor + jnp.sum(weights, axis=-1)
    accum = accum * factor[..., None] + jnp.einsum(
        "hst,thd->hsd", weights.astype(jnp.bfloat16), v_heads, preferred_element_type=jnp.float32
    )
    peak_now, totals, accum = (newest, totals, accum)
    attended = (accum / totals[..., None]).transpose(1, 0, 2).reshape(local_rows, model_width)
    mixed = resid[0].astype(jnp.float32) + attended
    mean_sq = jnp.mean(mixed * mixed, axis=-1, keepdims=True)
    normed = (mixed * lax.rsqrt(mean_sq + epsilon) * norm_gain).astype(jnp.bfloat16)
    owners = lax.axis_size("seq") * lax.axis_size("expert")
    groups = lax.axis_size("dp")
    capacity = 2 * local_rows // owners + 2
    zone_of = zone_ids[0, :, 0]
    expert_hot = (zone_of[:, None] == jnp.arange(owners, dtype=jnp.int32)[None, :]).astype(
        jnp.int32
    )
    ranking = jnp.cumsum(expert_hot, axis=0) - 1
    slot_index = jnp.sum(ranking * expert_hot, axis=1)
    target = zone_of * capacity + slot_index
    placing = (target[None, :] == jnp.arange(owners * capacity, dtype=jnp.int32)[:, None]).astype(
        jnp.bfloat16
    )
    send_x = jnp.dot(placing, normed, preferred_element_type=jnp.float32).astype(jnp.bfloat16)
    send_g = jnp.dot(placing, cotangent[0], preferred_element_type=jnp.float32).astype(jnp.bfloat16)
    send_x = send_x.reshape(owners, capacity, model_width)
    send_g = send_g.reshape(owners, capacity, model_width)
    row_x, row_g = (
        lax.all_to_all(send_x, ("seq", "expert"), split_axis=0, concat_axis=0, tiled=True),
        lax.all_to_all(send_g, ("seq", "expert"), split_axis=0, concat_axis=0, tiled=True),
    )
    arrived_x, arrived_g = (
        lax.all_gather(row_x, "dp", axis=0, tiled=True),
        lax.all_gather(row_g, "dp", axis=0, tiled=True),
    )
    slot_count = groups * owners * capacity
    inputs = arrived_x.reshape(slot_count, model_width)
    grads_in = arrived_g.reshape(slot_count, model_width)
    w_first = w_in[0]
    w_second = w_out[0]
    pre_act = jnp.dot(inputs, w_first, preferred_element_type=jnp.float32)
    activated, pull_back = jax.vjp(jax.nn.gelu, pre_act)
    hidden = activated.astype(jnp.bfloat16)
    back_proj = lax.dot_general(
        grads_in, w_second, (((1,), (1,)), ((), ())), preferred_element_type=jnp.float32
    )
    d_pre = pull_back(back_proj)[0].astype(jnp.bfloat16)
    grad_first = lax.dot_general(
        inputs, d_pre, (((0,), (0,)), ((), ())), preferred_element_type=jnp.float32
    ).astype(jnp.bfloat16)
    grad_second = lax.dot_general(
        hidden, grads_in, (((0,), (0,)), ((), ())), preferred_element_type=jnp.float32
    ).astype(jnp.bfloat16)
    summed = lax.psum_scatter(
        jnp.dot(hidden, w_second, preferred_element_type=jnp.float32).astype(jnp.bfloat16),
        "dp",
        scatter_dimension=0,
        tiled=True,
    )
    returned = lax.all_to_all(
        summed.reshape(owners, capacity, model_width),
        ("seq", "expert"),
        split_axis=0,
        concat_axis=0,
        tiled=True,
    )
    expert_rows = lax.dot_general(
        placing,
        returned.reshape(owners * capacity, model_width),
        (((0,), (0,)), ((), ())),
        preferred_element_type=jnp.float32,
    )
    layer_out = (mixed + expert_rows).astype(jnp.bfloat16)[None]
    return (layer_out, grad_first[None], grad_second[None])


def solution(mesh):
    placed = (
        P(("dp", "expert"), "seq", None),
        P(("dp", "expert"), "seq", None),
        P(("dp", "expert"), "seq", None),
        P(("dp", "expert"), "seq", None),
        P(("dp", "expert"), "seq", None),
        P(("dp", "expert"), "seq", None),
        P(),
        P(("seq", "expert"), None, "dp"),
        P(("seq", "expert"), "dp", None),
    )
    return jax.shard_map(
        shards,
        mesh=mesh,
        in_specs=placed,
        out_specs=(
            P(("dp", "expert"), "seq", None),
            P(("seq", "expert"), None, "dp"),
            P(("seq", "expert"), "dp", None),
        ),
        check_vma=False,
    )
```

profile of v0, /device:TPU:0, one launch (start us, length us, event | category | flops | bytes accessed | tf_op | source)
XLA Modules:
  0.0 370.8 jit_solution(17556214826301399096)
XLA Ops:
  7.2 0.0 all-gather.5.cloned.1.call-start
  7.2 2.1 copy.22
  9.3 0.0 all-gather.5.cloned.1.call-update
  9.3 0.0 all-gather.7.cloned.1.call-start
  9.4 0.7 all-gather.7.cloned.1.call-update
  10.1 0.0 all-gather.9.cloned.1.call-start
  10.1 1.1 copy.33
  11.3 2.2 copy.27
  13.5 0.1 fusion.42
  13.6 0.2 reduce_window_sum.11
  13.8 0.2 select_reduce_fusion
  14.0 45.2 %all-gather.5.cloned.1.call-done = bf16[1,512,2048]{1,2,0:T(8,128)(2,1)} async-done(((bf16[1,128,2048]{1,2,0:T(8,128)(2,1)}), bf16[1,512,2048]{1,2,0:T(8,128)(2,1)}) %all-gather.5.cloned.1.call-update) | async-done | bytes 2097168 | tf_op jit(solution)/shard_map/all_gather | solution.py:20
  59.2 2.4 multiply_reduce_fusion
  61.6 2.0 copy-done.2
  63.6 1.3 fusion.14
  64.9 39.7 %all-gather.7.cloned.1.call-done = bf16[1,512,2048]{2,1,0:T(8,128)(2,1)} async-done(((bf16[1,128,2048]{2,1,0:T(8,128)(2,1)}), bf16[1,512,2048]{2,1,0:T(8,128)(2,1)}) %all-gather.7.cloned.1.call-update) | async-done | bytes 2097168 | tf_op jit(solution)/shard_map/all_gather | solution.py:21
  104.6 2.9 copy.25
  107.5 4.7 %multiply_reduce_fusion.1 = (f32[128]{0:T(128)S(1)}, f32[128,16,128]{0,2,1:T(8,128)}) fusion(f32[128,16,128]{0,2,1:T(8,128)} %bitcast.59, f32[128,16]{0,1:T(8,128)S(1)} %bitcast_add_fusion.2, bf16[512,16,128]{0,2,1:T(8,128)(2,1)S(1)} %bitcast.56, f32[16,128,512]{2,1,0:T(8,128)} %copy-done.2, f32[16,128]{1,0:T(8,128)S(1)} %get-tuple-element.3, ...), kind=kOutput, calls=%fused_computation.34 | convolution fusion | flops 272891776 | bytes 8413696 | tf_op jit(solution)/shard_map/hst,thd->hsd/dot_general | solution.py:33
  112.2 1.6 copy.26
  113.8 1.5 convolution_convert_fusion.2
  115.3 1.4 reshape.62
  116.7 34.6 %all_to_all.15 = bf16[8,34,2048]{2,1,0:T(8,128)(2,1)S(1)} all-to-all(bf16[8,34,2048]{2,1,0:T(8,128)(2,1)S(1)} %reshape.62), channel_id=1, replica_groups=mesh['dp'=4,'seq'=4,'expert'=2] {'seq','expert'}, dimensions={0} | all-to-all | bytes 2228224 | tf_op jit(solution)/shard_map/all_to_all | solution.py:59
  151.3 1.6 copy.28
  153.0 0.0 all-gather.11.cloned.1.call-start
  153.0 1.4 convolution_convert_fusion.1
  154.5 1.4 reshape.66
  155.9 34.6 %all_to_all.16 = bf16[8,34,2048]{2,1,0:T(8,128)(2,1)S(1)} all-to-all(bf16[8,34,2048]{2,1,0:T(8,128)(2,1)S(1)} %reshape.66), channel_id=1, replica_groups=mesh['dp'=4,'seq'=4,'expert'=2] {'seq','expert'}, dimensions={0} | all-to-all | bytes 2228224 | tf_op jit(solution)/shard_map/all_to_all | solution.py:60
  190.5 1.6 copy.30
  192.1 0.0 all-gather.11.cloned.1.call-update
  192.1 0.0 reduce-scatter.2.cloned.1.call-start
  192.2 14.5 %all-gather.9.cloned.1.call-done = bf16[32,34,2048]{2,0,1:T(8,128)(2,1)} async-done(((bf16[8,34,2048]{2,0,1:T(8,128)(2,1)}), bf16[32,34,2048]{2,0,1:T(8,128)(2,1)}) %all-gather.9.cloned.1.call-update) | async-done | bytes 4456464 | tf_op jit(solution)/shard_map/all_gather | solution.py:63
  206.7 7.1 %copy.29 = bf16[32,34,2048]{2,1,0:T(8,128)(2,1)} copy(bf16[32,34,2048]{2,0,1:T(8,128)(2,1)} %all-gather.9.cloned.1.call-done) | data formatting | bytes 8912896 | tf_op jit(solution)/shard_map/all_gather | solution.py:63
  213.8 7.5 %reshape.63 = bf16[1088,2048]{1,0:T(8,128)(2,1)} reshape(bf16[32,34,2048]{2,1,0:T(8,128)(2,1)} %copy.29) | data formatting | bytes 8912896 | tf_op jit(solution)/shard_map/reshape | solution.py:67
  221.3 8.0 %fusion.12 = f32[1088,1024]{1,0:T(8,128)S(1)} fusion(bf16[1088,2048]{1,0:T(8,128)(2,1)} %reshape.63, bf16[1,2048,1024]{2,1,0:T(8,128)(2,1)} %param.16), kind=kOutput, calls=%fused_computation.14 | convolution fusion | flops 4563402752 | bytes 13107200 | tf_op jit(solution)/shard_map/dot_general | solution.py:71
  229.2 2.1 copy-done.7
  231.4 6.9 %convolution_convert_fusion = bf16[1088,2048]{1,0:T(8,128)(2,1)} fusion(bf16[1,1024,2048]{2,1,0:T(8,128)(2,1)S(1)} %copy-done.6, f32[1088,1024]{1,0:T(8,128)S(1)} %fusion.12), kind=kOutput, calls=%fused_computation | convolution fusion | flops 4575657984 | bytes 13107200 | tf_op jit(solution)/shard_map/dot_general | solution.py:85
  238.3 0.0 reduce-scatter.2.cloned.1.call-update
  238.3 25.5 %all-gather.11.cloned.1.call-done = bf16[32,34,2048]{2,0,1:T(8,128)(2,1)} async-done(((bf16[8,34,2048]{2,0,1:T(8,128)(2,1)}), bf16[32,34,2048]{2,0,1:T(8,128)(2,1)}) %all-gather.11.cloned.1.call-update) | async-done | bytes 4456464 | tf_op jit(solution)/shard_map/all_gather | solution.py:64
  263.8 7.1 %copy.31 = bf16[32,34,2048]{2,1,0:T(8,128)(2,1)} copy(bf16[32,34,2048]{2,0,1:T(8,128)(2,1)} %all-gather.11.cloned.1.call-done) | data formatting | bytes 8912896 | tf_op jit(solution)/shard_map/all_gather | solution.py:64
  270.8 7.4 %reshape.67 = bf16[1088,2048]{1,0:T(8,128)(2,1)} reshape(bf16[32,34,2048]{2,1,0:T(8,128)(2,1)} %copy.31) | data formatting | bytes 8912896 | tf_op jit(solution)/shard_map/reshape | solution.py:68
  278.3 10.7 %convert_bitcast_fusion = bf16[1,1024,2048]{2,1,0:T(8,128)(2,1)} fusion(bf16[1088,2048]{1,0:T(8,128)(2,1)} %reshape.67, f32[1088,1024]{1,0:T(8,128)} %copy-done.7), kind=kOutput, calls=%fused_computation.16 | convolution fusion | flops 4575526912 | bytes 13107200 | tf_op jit(solution)/shard_map/dot_general | solution.py:81
  289.0 32.5 %reduce-scatter.2.cloned.1.call-done = bf16[272,2048]{1,0:T(8,128)(2,1)} async-done(((bf16[1088,2048]{1,0:T(8,128)(2,1)}), bf16[272,2048]{1,0:T(8,128)(2,1)}) %reduce-scatter.2.cloned.1.call-update) | async-done | bytes 1114128 | tf_op jit(solution)/shard_map/reduce_scatter | solution.py:84
  321.5 2.3 reshape.64
  323.8 4.6 %all-to-all-start.1 = ((bf16[8,34,2048]{2,1,0:T(8,128)(2,1)}), bf16[8,34,2048]{2,1,0:T(8,128)(2,1)S(1)}, u32[]{:S(2)}, u32[]{:S(2)}) async-start(bf16[8,34,2048]{2,1,0:T(8,128)(2,1)} %reshape.64), calls=%async_computation.2 | async-start | bytes 2621440 | tf_op jit(solution)/shard_map/all_to_all | solution.py:90
  328.4 18.7 %convert_bitcast_fusion.1 = bf16[1,2048,1024]{2,1,0:T(8,128)(2,1)} fusion(bf16[1088,2048]{1,0:T(8,128)(2,1)} %reshape.63, f32[1088,1024]{1,0:T(8,128)} %copy-done.7, bf16[1088,2048]{1,0:T(8,128)(2,1)} %reshape.67, bf16[1,1024,2048]{2,1,0:T(8,128)(2,1)} %param.17), kind=kOutput, calls=%fused_computation.17 | convolution fusion | flops 9151184896 | bytes 21757952 | tf_op jit(solution)/shard_map/dot_general | solution.py:78
  347.1 13.5 %all-to-all-done.1 = bf16[8,34,2048]{2,1,0:T(8,128)(2,1)S(1)} async-done(((bf16[8,34,2048]{2,1,0:T(8,128)(2,1)}), bf16[8,34,2048]{2,1,0:T(8,128)(2,1)S(1)}, u32[]{:S(2)}, u32[]{:S(2)}) %all-to-all-start.1) | async-done | bytes 1114144 | tf_op jit(solution)/shard_map/all_to_all | solution.py:90
  360.6 1.2 reshape.65
  361.7 2.5 fusion.17
  (19 shorter events, 0.1 us)
Async XLA Ops:
  7.2 145.9 %copy-start = (bf16[1,128,2048]{2,1,0:T(8,128)(2,1)S(1)}, bf16[1,128,2048]{2,1,0:T(8,128)(2,1)}, u32[]{:S(2)}) copy-start(bf16[1,128,2048]{2,1,0:T(8,128)(2,1)} %param.13) | copy-start | bytes 1572868
  7.2 6.3 %copy-start.5 = (s32[1,128,1]{1,2,0:T(1,128)S(1)}, s32[1,128,1]{1,2,0:T(1,128)}, u32[]{:S(2)}) copy-start(s32[1,128,1]{1,2,0:T(1,128)} %param.14) | copy-start | bytes 1540
  7.2 52.0 %all-gather.5.cloned.1.call-start = ((), (), s32[]{:S(2)}) async-start(), calls=%async_computation.4 | async-start | bytes 2621440 | tf_op jit(solution)/shard_map/all_gather | solution.py:20
  9.3 95.2 %all-gather.7.cloned.1.call-start = ((), (), s32[]{:S(2)}) async-start(), calls=%async_computation.5 | async-start | bytes 2621440 | tf_op jit(solution)/shard_map/all_gather | solution.py:21
  10.1 196.6 %all-gather.9.cloned.1.call-start = ((), (), s32[]{:S(2)}) async-start(), calls=%async_computation.6 | async-start | bytes 5570560 | tf_op jit(solution)/shard_map/all_gather | solution.py:63
  61.5 2.0 copy-start.2
  107.5 6.3 %copy-start.3 = (bf16[1,128,2048]{2,1,0:T(8,128)(2,1)S(1)}, bf16[1,128,2048]{2,1,0:T(8,128)(2,1)}, u32[]{:S(2)}) copy-start(bf16[1,128,2048]{2,1,0:T(8,128)(2,1)} %param.12) | copy-start | bytes 1572868
  107.5 6.3 %copy-start.4 = (f32[2048]{0:T(1024)S(1)}, f32[2048]{0:T(1024)}, u32[]{:S(2)}) copy-start(f32[2048]{0:T(1024)} %param.15) | copy-start | bytes 24580
  153.0 110.8 %all-gather.11.cloned.1.call-start = ((), (), s32[]{:S(2)}) async-start(), calls=%async_computation.8 | async-start | bytes 5570560 | tf_op jit(solution)/shard_map/all_gather | solution.py:64
  192.1 129.4 %reduce-scatter.2.cloned.1.call-start = ((), (), s32[]{:S(2)}) async-start(), calls=%async_computation.7 | async-start | bytes 5570560 | tf_op jit(solution)/shard_map/reduce_scatter | solution.py:84
  221.3 10.1 %copy-start.6 = (bf16[1,1024,2048]{2,1,0:T(8,128)(2,1)S(1)}, bf16[1,1024,2048]{2,1,0:T(8,128)(2,1)}, u32[]{:S(2)}) copy-start(bf16[1,1024,2048]{2,1,0:T(8,128)(2,1)} %param.17) | copy-start | bytes 12582916
  229.2 2.1 copy-start.7
  323.8 36.8 %all-to-all-start.1 = ((bf16[8,34,2048]{2,1,0:T(8,128)(2,1)}), bf16[8,34,2048]{2,1,0:T(8,128)(2,1)S(1)}, u32[]{:S(2)}, u32[]{:S(2)}) async-start(bf16[8,34,2048]{2,1,0:T(8,128)(2,1)} %reshape.64), calls=%async_computation.2 | async-start | bytes 2621440 | tf_op jit(solution)/shard_map/all_to_all | solution.py:90
  328.4 35.9 %copy-start.1 = (bf16[1,128,2048]{2,1,0:T(8,128)(2,1)S(1)}, bf16[1,128,2048]{2,1,0:T(8,128)(2,1)}, u32[]{:S(2)}) copy-start(bf16[1,128,2048]{2,1,0:T(8,128)(2,1)} %param.13) | copy-start | bytes 1572868
Sparse Core Ops, SparseCore 0:
  10.1 48.9 all-gather.4
  60.7 43.8 all-gather.6
  153.1 53.5 all-gather.8
  209.0 54.7 all-gather.10
  266.7 54.7 reduce-scatter.1
where the time goes:
time: 372 us; the launch traced here: 371 us
  waiting for transfers between devices  172 us (46%)
  blocking collectives  69.2 us (19%)
  matrix products  56.8 us (15%)
  local copies, waits for them, and re-layouts  52.5 us (14%)
  between operations  13.9 us (4%)
  starting transfers between devices  4.81 us (1%)
    all_gather x1, waiting for transfers between devices, shards(): key_block = lax.all_gather(keys, 'seq', axis=1, tiled=True)  45.2 us
    all_gather x1, waiting for transfers between devices, shards(): value_block = lax.all_gather(values, 'seq', axis=1, tiled=True)  39.7 us
    all_to_all x1, blocking collectives, shards(): lax.all_to_all(send_x, ('seq', 'expert'), split_axis=0, concat_axis=0, ti...  34.6 us
    all_to_all x1, blocking collectives, shards(): lax.all_to_all(send_g, ('seq', 'expert'), split_axis=0, concat_axis=0, ti...  34.6 us
    reduce_scatter x1, waiting for transfers between devices, shards(): lax.psum_scatter(jnp.dot(hidden, w_second, preferred_element_type=jnp.flo...  32.5 us
    all_gather x1, waiting for transfers between devices, shards(): lax.all_gather(row_g, 'dp', axis=0, tiled=True)  25.5 us
    dot_general x1, matrix products, shards(): lax.dot_general(inputs, d_pre, (((0,), (0,)), ((), ())), preferred_elemen...  18.7 us
    all_gather x1, waiting for transfers between devices, shards(): lax.all_gather(row_x, 'dp', axis=0, tiled=True)  14.5 us
  transfers between devices with their start and end apart: 6, of which 6 were waited for; matrix products, arithmetic and copies ran while one was open for 23% of the time, Pallas kernels for 0%

commit v1 on v0

--- a/solution.py
+++ b/solution.py
@@ -17,7 +17,12 @@
     peak_now = jnp.full((HEADS, local_rows), -jnp.inf, jnp.float32)
     totals = jnp.zeros((HEADS, local_rows), jnp.float32)
     accum = jnp.zeros((HEADS, local_rows, head_dim), jnp.float32)
-    key_block = lax.all_gather(keys, "seq", axis=1, tiled=True)
+    ring = [keys]
+    for hop in range(3):
+        ring.append(lax.ppermute(ring[-1], "seq", [(dev, (dev + 1) % 4) for dev in range(4)]))
+    key_block = jnp.roll(
+        jnp.concatenate(ring[::-1], axis=1), (lax.axis_index("seq") + 1) * ring[0].shape[1], axis=1
+    )
     value_block = lax.all_gather(values, "seq", axis=1, tiled=True)
     count = key_block.shape[1]
     k_heads = key_block[0].reshape(count, HEADS, head_dim)

time: 372 us -> 353 us (0.949)
  waiting for transfers between devices: 172 us -> 151 us
    ppermute x0 -> x3, waiting for transfers between devices: none -> 52.6 us  [shards(): lax.ppermute(ring[-1], 'seq', [(dev, (dev + 1) % 4) for dev in range(4)])]
    all_gather x1 -> x0, waiting for transfers between devices: 45.2 us -> none  [shards(): key_block = lax.all_gather(keys, 'seq', axis=1, tiled=True)]
    all_gather x1, waiting for transfers between devices: 39.7 us -> 11.8 us  [shards(): value_block = lax.all_gather(values, 'seq', axis=1, tiled=True)]
    unnamed x18 -> x25, local copies, waits for them, and re-layouts: 7.4 us -> 7.87 us
  transfers between devices with their start and end apart: 6 -> 8, of which waited for: 6 -> 8; matrix products, arithmetic and copies ran while one was open for 23% -> 24% of each run, Pallas kernels for 0% -> 0%
where the time goes in v1:
time: 353 us; the launch traced here: 352 us
  waiting for transfers between devices  151 us (43%)
  blocking collectives  69.2 us (20%)
  matrix products  55.3 us (16%)
  local copies, waits for them, and re-layouts  53.4 us (15%)
  between operations  14 us (4%)
  starting transfers between devices  7.88 us (2%)
    ppermute x3, waiting for transfers between devices, shards(): lax.ppermute(ring[-1], 'seq', [(dev, (dev + 1) % 4) for dev in range(4)])  52.6 us
    all_to_all x1, blocking collectives, shards(): lax.all_to_all(send_x, ('seq', 'expert'), split_axis=0, concat_axis=0, ti...  34.6 us
    all_to_all x1, blocking collectives, shards(): lax.all_to_all(send_g, ('seq', 'expert'), split_axis=0, concat_axis=0, ti...  34.6 us
    reduce_scatter x1, waiting for transfers between devices, shards(): lax.psum_scatter(jnp.dot(hidden, w_second, preferred_element_type=jnp.flo...  32.5 us
    all_gather x1, waiting for transfers between devices, shards(): lax.all_gather(row_g, 'dp', axis=0, tiled=True)  25.8 us
    dot_general x1, matrix products, shards(): lax.dot_general(inputs, d_pre, (((0,), (0,)), ((), ())), preferred_elemen...  18.7 us
    all_gather x1, waiting for transfers between devices, shards(): lax.all_gather(row_x, 'dp', axis=0, tiled=True)  14.4 us
    all_to_all x1, waiting for transfers between devices, shards(): lax.all_to_all(summed.reshape(owners, capacity, model_width), ('seq', 'ex...  13.5 us
  transfers between devices with their start and end apart: 8, of which 8 were waited for; matrix products, arithmetic and copies ran while one was open for 24% of the time, Pallas kernels for 0%

profile of v1, /device:TPU:0, one launch (start us, length us, event | category | flops | bytes accessed | tf_op | source)
XLA Modules:
  0.0 352.3 jit_solution(2901848132763800016)
XLA Ops:
  7.2 1.4 copy.26
  8.6 3.1 collective-permute-start
  11.7 13.9 %collective-permute-done = bf16[1,128,2048]{1,2,0:T(8,128)(2,1)S(1)} collective-permute-done((bf16[1,128,2048]{1,2,0:T(8,128)(2,1)S(1)}, bf16[1,128,2048]{1,2,0:T(8,128)(2,1)S(1)}, u32[]{:S(2)}, u32[]{:S(2)}) %collective-permute-start) | collective-permute-done | bytes 524320 | tf_op jit(solution)/shard_map/ppermute | solution.py:22
  25.7 16.8 %collective-permute-done.1 = bf16[1,128,2048]{1,2,0:T(8,128)(2,1)S(1)} collective-permute-done((bf16[1,128,2048]{1,2,0:T(8,128)(2,1)S(1)}, bf16[1,128,2048]{1,2,0:T(8,128)(2,1)S(1)}, u32[]{:S(2)}, u32[]{:S(2)}) %collective-permute-start.1) | collective-permute-done | bytes 524320 | tf_op jit(solution)/shard_map/ppermute | solution.py:22
  42.5 0.7 fusion.43
  43.4 1.1 copy.41
  44.6 2.2 copy.34
  47.0 21.9 %collective-permute-done.2 = bf16[1,128,2048]{1,2,0:T(8,128)(2,1)S(1)} collective-permute-done((bf16[1,128,2048]{1,2,0:T(8,128)(2,1)S(1)}, bf16[1,128,2048]{1,2,0:T(8,128)(2,1)S(1)}, u32[]{:S(2)}, u32[]{:S(2)}) %collective-permute-start.2) | collective-permute-done | bytes 524320 | tf_op jit(solution)/shard_map/ppermute | solution.py:22
  69.0 0.2 constant_dynamic-update-slice_fusion.6
  69.2 0.2 constant_dynamic-update-slice_fusion.5
  69.4 0.2 constant_dynamic-update-slice_fusion.4
  69.6 0.2 constant_dynamic-update-slice_fusion.3
  69.8 0.2 constant_dynamic-update-slice_fusion.2
  70.0 0.2 constant_dynamic-update-slice_fusion.1
  70.1 0.2 constant_dynamic-update-slice_fusion
  70.3 0.2 constant_dynamic-slice_fusion
  70.6 0.9 bitcast_reduce_fusion
  71.6 2.0 copy-done.2
  73.5 0.7 fusion.15
  74.3 11.8 %all-gather.4.cloned.1.call-done = bf16[1,512,2048]{2,1,0:T(8,128)(2,1)} async-done(((bf16[1,128,2048]{2,1,0:T(8,128)(2,1)}), bf16[1,512,2048]{2,1,0:T(8,128)(2,1)}) %all-gather.4.cloned.1.call-update) | async-done | bytes 2097168 | tf_op jit(solution)/shard_map/all_gather | solution.py:26
  86.1 2.9 copy.31
  89.0 4.7 %multiply_reduce_fusion = (f32[128]{0:T(128)S(1)}, f32[128,16,128]{0,2,1:T(8,128)}) fusion(f32[128,16,128]{0,2,1:T(8,128)} %bitcast.77, f32[128,16]{0,1:T(8,128)S(1)} %bitcast_add_fusion.2, bf16[512,16,128]{0,2,1:T(8,128)(2,1)S(1)} %bitcast.75, f32[16,512,128]{2,1,0:T(8,128)} %copy-done.2, f32[16,128]{1,0:T(8,128)S(1)} %get-tuple-element.3, ...), kind=kOutput, calls=%fused_computation.35 | convolution fusion | flops 272891776 | bytes 8413696 | tf_op jit(solution)/shard_map/hst,thd->hsd/dot_general | solution.py:38
  93.7 1.6 copy.33
  95.3 1.5 convolution_convert_fusion.2
  96.8 1.4 reshape.62
  98.2 34.6 %all_to_all.15 = bf16[8,34,2048]{2,1,0:T(8,128)(2,1)S(1)} all-to-all(bf16[8,34,2048]{2,1,0:T(8,128)(2,1)S(1)} %reshape.62), channel_id=1, replica_groups=mesh['dp'=4,'seq'=4,'expert'=2] {'seq','expert'}, dimensions={0} | all-to-all | bytes 2228224 | tf_op jit(solution)/shard_map/all_to_all | solution.py:64
  132.8 1.6 copy.35
  134.5 1.4 convolution_convert_fusion.1
  136.0 1.4 reshape.66
  137.4 34.6 %all_to_all.16 = bf16[8,34,2048]{2,1,0:T(8,128)(2,1)S(1)} all-to-all(bf16[8,34,2048]{2,1,0:T(8,128)(2,1)S(1)} %reshape.66), channel_id=1, replica_groups=mesh['dp'=4,'seq'=4,'expert'=2] {'seq','expert'}, dimensions={0} | all-to-all | bytes 2228224 | tf_op jit(solution)/shard_map/all_to_all | solution.py:65
  172.0 1.6 copy.37
  173.7 14.4 %all-gather.6.cloned.1.call-done = bf16[32,34,2048]{2,0,1:T(8,128)(2,1)} async-done(((bf16[8,34,2048]{2,0,1:T(8,128)(2,1)}), bf16[32,34,2048]{2,0,1:T(8,128)(2,1)}) %all-gather.6.cloned.1.call-update) | async-done | bytes 4456464 | tf_op jit(solution)/shard_map/all_gather | solution.py:68
  188.1 7.1 %copy.36 = bf16[32,34,2048]{2,1,0:T(8,128)(2,1)} copy(bf16[32,34,2048]{2,0,1:T(8,128)(2,1)} %all-gather.6.cloned.1.call-done) | data formatting | bytes 8912896 | tf_op jit(solution)/shard_map/all_gather | solution.py:68
  195.2 7.4 %reshape.63 = bf16[1088,2048]{1,0:T(8,128)(2,1)} reshape(bf16[32,34,2048]{2,1,0:T(8,128)(2,1)} %copy.36) | data formatting | bytes 8912896 | tf_op jit(solution)/shard_map/reshape | solution.py:72
  202.6 8.0 %fusion.12 = f32[1088,1024]{1,0:T(8,128)S(1)} fusion(bf16[1088,2048]{1,0:T(8,128)(2,1)} %reshape.63, bf16[1,2048,1024]{2,1,0:T(8,128)(2,1)} %param.16), kind=kOutput, calls=%fused_computation.14 | convolution fusion | flops 4563402752 | bytes 13107200 | tf_op jit(solution)/shard_map/dot_general | solution.py:76
  210.6 2.1 copy-done.7
  212.7 6.7 %convolution_convert_fusion = bf16[1088,2048]{1,0:T(8,128)(2,1)} fusion(bf16[1,1024,2048]{2,1,0:T(8,128)(2,1)S(1)} %copy-done.6, f32[1088,1024]{1,0:T(8,128)S(1)} %fusion.12), kind=kOutput, calls=%fused_computation | convolution fusion | flops 4575657984 | bytes 13107200 | tf_op jit(solution)/shard_map/dot_general | solution.py:90
  219.5 25.8 %all-gather.8.cloned.1.call-done = bf16[32,34,2048]{2,0,1:T(8,128)(2,1)} async-done(((bf16[8,34,2048]{2,0,1:T(8,128)(2,1)}), bf16[32,34,2048]{2,0,1:T(8,128)(2,1)}) %all-gather.8.cloned.1.call-update) | async-done | bytes 4456464 | tf_op jit(solution)/shard_map/all_gather | solution.py:69
  245.3 7.1 %copy.38 = bf16[32,34,2048]{2,1,0:T(8,128)(2,1)} copy(bf16[32,34,2048]{2,0,1:T(8,128)(2,1)} %all-gather.8.cloned.1.call-done) | data formatting | bytes 8912896 | tf_op jit(solution)/shard_map/all_gather | solution.py:69
  252.4 7.4 %reshape.67 = bf16[1088,2048]{1,0:T(8,128)(2,1)} reshape(bf16[32,34,2048]{2,1,0:T(8,128)(2,1)} %copy.38) | data formatting | bytes 8912896 | tf_op jit(solution)/shard_map/reshape | solution.py:73
  259.8 10.7 %convert_bitcast_fusion = bf16[1,1024,2048]{2,1,0:T(8,128)(2,1)} fusion(bf16[1088,2048]{1,0:T(8,128)(2,1)} %reshape.67, f32[1088,1024]{1,0:T(8,128)} %copy-done.7), kind=kOutput, calls=%fused_computation.19 | convolution fusion | flops 4575526912 | bytes 13107200 | tf_op jit(solution)/shard_map/dot_general | solution.py:86
  270.5 32.5 %reduce-scatter.2.cloned.1.call-done = bf16[272,2048]{1,0:T(8,128)(2,1)} async-done(((bf16[1088,2048]{1,0:T(8,128)(2,1)}), bf16[272,2048]{1,0:T(8,128)(2,1)}) %reduce-scatter.2.cloned.1.call-update) | async-done | bytes 1114128 | tf_op jit(solution)/shard_map/reduce_scatter | solution.py:89
  303.0 2.3 reshape.64
  305.3 4.6 %all-to-all-start.1 = ((bf16[8,34,2048]{2,1,0:T(8,128)(2,1)}), bf16[8,34,2048]{2,1,0:T(8,128)(2,1)S(1)}, u32[]{:S(2)}, u32[]{:S(2)}) async-start(bf16[8,34,2048]{2,1,0:T(8,128)(2,1)} %reshape.64), calls=%async_computation.2 | async-start | bytes 2621440 | tf_op jit(solution)/shard_map/all_to_all | solution.py:95
  309.9 18.7 %convert_bitcast_fusion.1 = bf16[1,2048,1024]{2,1,0:T(8,128)(2,1)} fusion(bf16[1088,2048]{1,0:T(8,128)(2,1)} %reshape.63, f32[1088,1024]{1,0:T(8,128)} %copy-done.7, bf16[1088,2048]{1,0:T(8,128)(2,1)} %reshape.67, bf16[1,1024,2048]{2,1,0:T(8,128)(2,1)} %param.17), kind=kOutput, calls=%fused_computation.20 | convolution fusion | flops 9151184896 | bytes 21757952 | tf_op jit(solution)/shard_map/dot_general | solution.py:83
  328.6 13.5 %all-to-all-done.1 = bf16[8,34,2048]{2,1,0:T(8,128)(2,1)S(1)} async-done(((bf16[8,34,2048]{2,1,0:T(8,128)(2,1)}), bf16[8,34,2048]{2,1,0:T(8,128)(2,1)S(1)}, u32[]{:S(2)}, u32[]{:S(2)}) %all-to-all-start.1) | async-done | bytes 1114144 | tf_op jit(solution)/shard_map/all_to_all | solution.py:95
  342.1 1.2 reshape.65
  343.3 2.5 fusion.18
  (31 shorter events, 0.8 us)
Async XLA Ops:
  7.2 127.4 %copy-start = (bf16[1,128,2048]{2,1,0:T(8,128)(2,1)S(1)}, bf16[1,128,2048]{2,1,0:T(8,128)(2,1)}, u32[]{:S(2)}) copy-start(bf16[1,128,2048]{2,1,0:T(8,128)(2,1)} %param.13) | copy-start | bytes 1572868
  7.2 39.6 %copy-start.5 = (s32[1,128,1]{1,2,0:T(1,128)S(1)}, s32[1,128,1]{1,2,0:T(1,128)}, u32[]{:S(2)}) copy-start(s32[1,128,1]{1,2,0:T(1,128)} %param.14) | copy-start | bytes 1540
  7.2 78.9 %all-gather.4.cloned.1.call-start = ((), (), s32[]{:S(2)}) async-start(), calls=%async_computation.4 | async-start | bytes 2621440 | tf_op jit(solution)/shard_map/all_gather | solution.py:26
  8.6 17.1 %collective-permute-start = (bf16[1,128,2048]{1,2,0:T(8,128)(2,1)S(1)}, bf16[1,128,2048]{1,2,0:T(8,128)(2,1)S(1)}, u32[]{:S(2)}, u32[]{:S(2)}) collective-permute-start(bf16[1,128,2048]{1,2,0:T(8,128)(2,1)S(1)} %copy.26), channel_id=1, source_target_pairs={{0,2},{2,4},{4,6},{6,0},{1,3},{3,5},{5,7},{7,1},{8,10},{10,12},{12... | collective-permute-start | bytes 1572872 | tf_op jit(solution)/shard_map/ppermute | solution.py:22
  25.7 16.9 %collective-permute-start.1 = (bf16[1,128,2048]{1,2,0:T(8,128)(2,1)S(1)}, bf16[1,128,2048]{1,2,0:T(8,128)(2,1)S(1)}, u32[]{:S(2)}, u32[]{:S(2)}) collective-permute-start(bf16[1,128,2048]{1,2,0:T(8,128)(2,1)S(1)} %collective-permute-done), channel_id=1, source_target_pairs={{0,2},{2,4},{4,6},{6,0},{1,3},{3,5},{5,7},{7,1},{8,10},{10,12},{12... | collective-permute-start | bytes 1572872 | tf_op jit(solution)/shard_map/ppermute | solution.py:22
  25.7 162.4 %all-gather.6.cloned.1.call-start = ((), (), s32[]{:S(2)}) async-start(), calls=%async_computation.5 | async-start | bytes 5570560 | tf_op jit(solution)/shard_map/all_gather | solution.py:68
  42.5 26.4 %collective-permute-start.2 = (bf16[1,128,2048]{1,2,0:T(8,128)(2,1)S(1)}, bf16[1,128,2048]{1,2,0:T(8,128)(2,1)S(1)}, u32[]{:S(2)}, u32[]{:S(2)}) collective-permute-start(bf16[1,128,2048]{1,2,0:T(8,128)(2,1)S(1)} %collective-permute-done.1), channel_id=1, source_target_pairs={{0,2},{2,4},{4,6},{6,0},{1,3},{3,5},{5,7},{7,1},{8,10},{10,12},{12... | collective-permute-start | bytes 1572872 | tf_op jit(solution)/shard_map/ppermute | solution.py:22
  71.5 2.0 copy-start.2
  89.0 6.3 %copy-start.3 = (bf16[1,128,2048]{2,1,0:T(8,128)(2,1)S(1)}, bf16[1,128,2048]{2,1,0:T(8,128)(2,1)}, u32[]{:S(2)}) copy-start(bf16[1,128,2048]{2,1,0:T(8,128)(2,1)} %param.12) | copy-start | bytes 1572868
  89.0 6.3 %copy-start.4 = (f32[2048]{0:T(1024)S(1)}, f32[2048]{0:T(1024)}, u32[]{:S(2)}) copy-start(f32[2048]{0:T(1024)} %param.15) | copy-start | bytes 24580
  134.5 110.8 %all-gather.8.cloned.1.call-start = ((), (), s32[]{:S(2)}) async-start(), calls=%async_computation.7 | async-start | bytes 5570560 | tf_op jit(solution)/shard_map/all_gather | solution.py:69
  173.6 129.4 %reduce-scatter.2.cloned.1.call-start = ((), (), s32[]{:S(2)}) async-start(), calls=%async_computation.6 | async-start | bytes 5570560 | tf_op jit(solution)/shard_map/reduce_scatter | solution.py:89
  202.6 10.1 %copy-start.6 = (bf16[1,1024,2048]{2,1,0:T(8,128)(2,1)S(1)}, bf16[1,1024,2048]{2,1,0:T(8,128)(2,1)}, u32[]{:S(2)}) copy-start(bf16[1,1024,2048]{2,1,0:T(8,128)(2,1)} %param.17) | copy-start | bytes 12582916
  210.6 2.1 copy-start.7
  305.3 36.8 %all-to-all-start.1 = ((bf16[8,34,2048]{2,1,0:T(8,128)(2,1)}), bf16[8,34,2048]{2,1,0:T(8,128)(2,1)S(1)}, u32[]{:S(2)}, u32[]{:S(2)}) async-start(bf16[8,34,2048]{2,1,0:T(8,128)(2,1)} %reshape.64), calls=%async_computation.2 | async-start | bytes 2621440 | tf_op jit(solution)/shard_map/all_to_all | solution.py:95
  309.9 35.9 %copy-start.1 = (bf16[1,128,2048]{2,1,0:T(8,128)(2,1)S(1)}, bf16[1,128,2048]{2,1,0:T(8,128)(2,1)}, u32[]{:S(2)}) copy-start(bf16[1,128,2048]{2,1,0:T(8,128)(2,1)} %param.13) | copy-start | bytes 1572868
Sparse Core Ops, SparseCore 0:
  25.8 60.2 all-gather.3
  134.6 53.4 all-gather.5
  190.5 54.7 all-gather.7
  248.2 54.7 reduce-scatter.1
